TPU v7x, 32 devices: a whole 2x2x4 slice. The times are simulated.
32 devices in a mesh: dp: 8 (over y, x, core), mp: 4 (over z).
Axes of the slice: x: 2, y: 2, z: 4, core: 2. Of those that a mesh axis runs over, the one named last changes fastest.
Arguments:
- patches: bfloat16 [8192, 1024], P(('dp', 'mp')), as said below
- scene_ids: int32 [8192], P(('dp', 'mp')), may hold values from 0 to 7, as said below
- owner_ids: int32 [8192], P(('dp', 'mp')), may hold values from 0 to 7, as said below
- fill_slot: int32 [32768], P(('dp', 'mp')), may hold values from -1 to 511, as said below
- norm1_gain: float32 [1024], replicated, may hold values from 0.1 to 1.9
- norm1_bias: float32 [1024], replicated, may hold values from -1.75 to 1.75
- qkv_weight: bfloat16 [1024, 3, 1024], P(None, None, 'mp'), may hold values from -0.25 to 0.25
- qv_bias: float32 [2, 1024], P(None, 'mp'), may hold values from -3 to 3
- out_weight: bfloat16 [1024, 1024], P('mp'), may hold values from -1.5 to 1.5
- out_bias: float32 [1024], replicated, may hold values from -1.75 to 1.75
- norm2_gain: float32 [1024], replicated, may hold values from 0.1 to 1.9
- norm2_bias: float32 [1024], replicated, may hold values from -1.75 to 1.75
- up_weight: bfloat16 [1024, 4096], P(None, 'mp'), may hold values from -0.1875 to 0.1875
- up_bias: bfloat16 [4096], P('mp'), may hold values from -3 to 3
- down_weight: bfloat16 [4096, 1024], P('mp'), may hold values from -0.125 to 0.125
- down_bias: float32 [1024], replicated, may hold values from -1.75 to 1.75
- dec_weight: bfloat16 [1024, 512], replicated, may hold values from -0.1875 to 0.1875
- dec_bias: float32 [512], replicated, may hold values from -1.75 to 1.75
- mask_token: float32 [512], replicated, may hold values from -6 to 6
- positions: bfloat16 [32768, 512], P(('dp', 'mp')), may hold values from -6 to 6
- cotangent: bfloat16 [32768, 512], P(('dp', 'mp')), may hold values from -6 to 6
Outputs:
- decoder_in: bfloat16 [32768, 512], P(('dp', 'mp'))
- grad_patches: float32 [8192, 1024], P(('dp', 'mp'))
- grad_norm1_gain: float32 [1024], replicated
- grad_norm1_bias: float32 [1024], replicated
- grad_qkv_weight: float32 [1024, 3, 1024], P(None, None, 'mp')
- grad_qv_bias: float32 [2, 1024], P(None, 'mp')
- grad_out_weight: float32 [1024, 1024], P('mp')
- grad_out_bias: float32 [1024], replicated
- grad_norm2_gain: float32 [1024], replicated
- grad_norm2_bias: float32 [1024], replicated
- grad_up_weight: float32 [1024, 4096], P(None, 'mp')
- grad_up_bias: float32 [4096], P('mp')
- grad_down_weight: float32 [4096, 1024], P('mp')
- grad_down_bias: float32 [1024], replicated
- grad_dec_weight: float32 [1024, 512], replicated
- grad_dec_bias: float32 [512], replicated
- grad_mask_token: float32 [512], replicated
Inputs may be any that keep to these rules, and one draw needn't show every extreme that they name: `scene_ids`: within each group of 1024 rows (one dp index) scene ids start at 0 and rise by one at each scene boundary, never falling; scene 0 holds 256 to 512 rows, every other scene at least one. `owner_ids`: among the 256 rows of one device no owner is named more than 64 times; in each mp column one owner is named exactly 64 times by the rows of every device. `fill_slot`: in grid block e, slot s * 64 + r is named by exactly one cell when device (s, e % 4) has an r-th row (in row order) with owner e // 4, and by no cell otherwise. `patches`: magnitudes stay below 200.
All inputs are finite; a program needn't handle non-finite values.
Results may differ from a plain program's by a relative error of at most 0.013.
The roundings to bfloat16 on the way count: a program that leaves them out, or rounds other values in their place, can miss the bound.
Values may be sent and summed in bfloat16 or wider, within the bound.
A program may use at most 128 MiB of HBM per device.

v0:
```python
import jax
import jax.numpy as jnp
from jax import lax
from jax.sharding import PartitionSpec as P

HEAD_DIM = 64
QBLOCK = 512
NEG_FILL = -1000000000.0


def layer_norm(hidden, gain, bias_vec):
    centered = hidden - jnp.mean(hidden, axis=-1, keepdims=True)
    spread = jnp.mean(centered * centered, axis=-1, keepdims=True)
    return centered * lax.rsqrt(spread + 1e-06) * gain + bias_vec


def gelu_exact(values):
    return jax.nn.gelu(values, approximate=False)


def gather_rows(weight, data_par, model_par):
    rows, width = weight.shape
    part = rows // data_par
    mine = lax.dynamic_slice_in_dim(weight, lax.axis_index("dp") * part, part, 0)
    column = lax.all_gather(mine, "mp", axis=0)
    whole = lax.all_gather(column, "dp", axis=0)
    return whole.transpose(1, 0, 2, 3).reshape(model_par * rows, width)


def low(values):
    return values.astype(jnp.bfloat16)


def per_device(
    patches,
    scene_ids,
    owner_ids,
    fill_slot,
    norm1_gain,
    norm1_bias,
    qkv_weight,
    qv_bias,
    out_weight,
    out_bias,
    norm2_gain,
    norm2_bias,
    up_weight,
    up_bias,
    down_weight,
    down_bias,
    dec_weight,
    dec_bias,
    mask_token,
    positions,
    cotangent,
):
    row_count = patches.shape[0]
    model_par = lax.axis_size("mp")
    data_par = lax.axis_size("dp")
    group_rows = row_count * model_par
    total_rows = float(row_count * model_par * data_par)
    local_width = qkv_weight.shape[2]
    local_heads = local_width // HEAD_DIM
    score_scale = HEAD_DIM ** (-0.5)
    block_rows = min(QBLOCK, group_rows)
    block_starts = jnp.arange(group_rows // block_rows, dtype=jnp.int32) * block_rows
    capacity = 2 * row_count // data_par
    slot_count = capacity * data_par
    dec_width = dec_weight.shape[1]
    out_full = gather_rows(out_weight, data_par, model_par)
    inputs_f = patches.astype(jnp.float32)
    band_sums = lax.psum(
        (jnp.sum(inputs_f, axis=0), jnp.sum(inputs_f * inputs_f, axis=0)), ("dp", "mp")
    )
    band_mean = band_sums[0] / total_rows
    band_var = band_sums[1] / total_rows - band_mean * band_mean
    band_scale = lax.rsqrt(band_var + 1e-05)
    band_hat = (inputs_f - band_mean) * band_scale
    normed1 = layer_norm(band_hat, norm1_gain, norm1_bias).astype(jnp.bfloat16)
    norm1_all, scene_all = (
        lax.all_gather(normed1, "mp", axis=0, tiled=True),
        lax.all_gather(scene_ids, "mp", axis=0, tiled=True),
    )
    bias_three = jnp.stack([qv_bias[0], jnp.zeros_like(qv_bias[0]), qv_bias[1]])
    triples = (
        jnp.einsum("td,dcj->tcj", norm1_all, qkv_weight, preferred_element_type=jnp.float32)
        + bias_three
    ).astype(jnp.bfloat16)
    query_all = triples[:, 0].reshape(group_rows, local_heads, HEAD_DIM)
    key_all = triples[:, 1].reshape(group_rows, local_heads, HEAD_DIM)
    value_all = triples[:, 2].reshape(group_rows, local_heads, HEAD_DIM)

    def block_scores(first_row):
        query_blk = lax.dynamic_slice_in_dim(query_all, first_row, block_rows, 0)
        scene_blk = lax.dynamic_slice_in_dim(scene_all, first_row, block_rows, 0)
        scores = (
            jnp.einsum("qhd,khd->hqk", query_blk, key_all, preferred_element_type=jnp.float32)
            * score_scale
        )
        same_scene = (scene_blk[:, None] == scene_all[None, :])[None]
        return (jnp.where(same_scene, scores, NEG_FILL), query_blk)

    def attend_block(first_row):
        scores, query_blk = block_scores(first_row)
        row_max = jnp.max(scores, axis=-1, keepdims=True)
        exp_scores = jnp.exp(scores - row_max)
        row_total = jnp.sum(exp_scores, axis=-1, keepdims=True)
        softmax_w = (exp_scores / row_total).astype(jnp.bfloat16)
        mixed_rows = jnp.einsum(
            "hqk,khd->qhd", softmax_w, value_all, preferred_element_type=jnp.float32
        )
        return (mixed_rows.astype(jnp.bfloat16), (row_max + jnp.log(row_total))[..., 0])

    head_blocks, lse_blocks = lax.map(attend_block, block_starts)
    heads_out = head_blocks.reshape(group_rows, local_width)
    heads_rows = lax.all_to_all(heads_out, "mp", split_axis=0, concat_axis=1, tiled=True)
    attn_local = jnp.dot(heads_rows, out_full, preferred_element_type=jnp.float32)
    after_attn = band_hat + attn_local + out_bias
    normed2 = layer_norm(after_attn, norm2_gain, norm2_bias).astype(jnp.bfloat16)
    norm2_all = lax.all_gather(normed2, "mp", axis=0, tiled=True)
    pre_act = jnp.dot(norm2_all, up_weight, preferred_element_type=jnp.float32) + up_bias.astype(
        jnp.float32
    )
    act_rows = gelu_exact(pre_act).astype(jnp.bfloat16)
    mlp_part = low(jnp.dot(act_rows, down_weight, preferred_element_type=jnp.float32))
    proj_part = jnp.dot(mlp_part, dec_weight, preferred_element_type=jnp.float32)
    proj_sum = lax.psum_scatter(low(proj_part), "mp", scatter_dimension=0, tiled=True)
    direct = after_attn + down_bias
    projected = low(
        jnp.dot(low(direct), dec_weight, preferred_element_type=jnp.float32)
        + proj_sum.astype(jnp.float32)
        + dec_bias
    )
    owner_onehot = (owner_ids[:, None] == jnp.arange(data_par, dtype=jnp.int32)[None, :]).astype(
        jnp.int32
    )
    earlier = jnp.sum((jnp.cumsum(owner_onehot, axis=0) - owner_onehot) * owner_onehot, axis=1)
    send_slot = owner_ids * capacity + earlier
    slot_range = jnp.arange(slot_count, dtype=jnp.int32)
    send_onehot = (send_slot[:, None] == slot_range[None, :]).astype(jnp.bfloat16)
    outgoing = jnp.einsum(
        "rs,rc->sc", send_onehot, projected, preferred_element_type=jnp.float32
    ).astype(jnp.bfloat16)
    fill_onehot = (fill_slot[:, None] == slot_range[None, :]).astype(jnp.bfloat16)
    returning = jnp.einsum(
        "gs,gc->sc", fill_onehot, cotangent, preferred_element_type=jnp.float32
    ).astype(jnp.bfloat16)
    arrived, grad_back = (
        lax.all_to_all(
            outgoing.reshape(data_par, capacity, dec_width),
            "dp",
            split_axis=0,
            concat_axis=0,
            tiled=True,
        ),
        lax.all_to_all(
            returning.reshape(data_par, capacity, dec_width),
            "dp",
            split_axis=0,
            concat_axis=0,
            tiled=True,
        ),
    )
    placed = jnp.dot(
        fill_onehot, arrived.reshape(slot_count, dec_width), preferred_element_type=jnp.float32
    )
    masked = (fill_slot < 0)[:, None]
    decoder_in = (jnp.where(masked, mask_token, placed) + positions.astype(jnp.float32)).astype(
        jnp.bfloat16
    )
    grad_mask_local = jnp.sum(jnp.where(masked, cotangent.astype(jnp.float32), 0.0), axis=0)
    grad_proj = jnp.einsum(
        "rs,sc->rc",
        send_onehot,
        grad_back.reshape(slot_count, dec_width),
        preferred_element_type=jnp.float32,
    )
    grad_proj_low = grad_proj.astype(jnp.bfloat16)
    proj_grad_all = lax.all_gather(grad_proj_low, "mp", axis=0, tiled=True)
    grad_dec_local = jnp.einsum(
        "rd,rc->dc", low(direct), grad_proj_low, preferred_element_type=jnp.float32
    ) + jnp.einsum("rd,rc->dc", mlp_part, proj_grad_all, preferred_element_type=jnp.float32)
    grad_dec_bias_local = jnp.sum(grad_proj, axis=0)
    grad_block = jnp.einsum(
        "rc,dc->rd", grad_proj_low, dec_weight, preferred_element_type=jnp.float32
    )
    grad_down_bias_local = jnp.sum(low(grad_block).astype(jnp.float32), axis=0)
    grad_mlp_all = low(
        jnp.einsum("rc,dc->rd", proj_grad_all, dec_weight, preferred_element_type=jnp.float32)
    )
    grad_act = jnp.einsum(
        "tc,fc->tf", grad_mlp_all, down_weight, preferred_element_type=jnp.float32
    )
    grad_down_local = jnp.einsum(
        "tf,tc->fc", act_rows, grad_mlp_all, preferred_element_type=jnp.float32
    )
    down_sum = lax.psum(low(grad_down_local), "dp").astype(jnp.float32)
    gelu_val, gelu_back = jax.vjp(gelu_exact, pre_act)
    grad_pre = gelu_back(grad_act)[0].astype(jnp.bfloat16)
    grad_up_local = jnp.einsum("td,tf->df", norm2_all, grad_pre, preferred_element_type=jnp.float32)
    grad_up_bias_local = jnp.sum(grad_pre.astype(jnp.float32), axis=0)
    grad_norm2 = lax.psum_scatter(
        low(jnp.einsum("tf,df->td", grad_pre, up_weight, preferred_element_type=jnp.float32)),
        "mp",
        scatter_dimension=0,
        tiled=True,
    ).astype(jnp.float32)
    up_sum = lax.psum(low(grad_up_local), "dp").astype(jnp.float32)
    norm2_val, norm2_back = jax.vjp(layer_norm, after_attn, norm2_gain, norm2_bias)
    from_norm2, grad_gain2_local, grad_bias2_local = norm2_back(grad_norm2)
    grad_after = grad_block + from_norm2
    grad_attn = grad_after.astype(jnp.bfloat16)
    grad_out_bias_local = jnp.sum(grad_attn.astype(jnp.float32), axis=0)
    grad_out_rows = low(
        jnp.einsum("tj,tc->jc", heads_rows, grad_attn, preferred_element_type=jnp.float32)
    ).reshape(model_par, local_width, -1)
    out_part = lax.psum_scatter(grad_out_rows, "dp", scatter_dimension=1, tiled=True)
    out_part = lax.psum_scatter(out_part, "mp", scatter_dimension=0, tiled=True)
    out_sum = lax.all_gather(out_part[0], "dp", axis=0, tiled=True).astype(jnp.float32)
    grad_heads = lax.all_to_all(
        low(jnp.einsum("tc,jc->tj", grad_attn, out_full, preferred_element_type=jnp.float32)),
        "mp",
        split_axis=1,
        concat_axis=0,
        tiled=True,
    )
    grad_heads3 = grad_heads.reshape(group_rows, local_heads, HEAD_DIM)

    def back_block(carried, inputs):
        key_acc, value_acc = carried
        first_row, log_total = inputs
        scores, query_blk = block_scores(first_row)
        softmax_w = jnp.exp(scores - log_total[..., None])
        upstream = lax.dynamic_slice_in_dim(grad_heads3, first_row, block_rows, 0)
        value_acc = value_acc + jnp.einsum(
            "hqk,qhd->khd",
            softmax_w.astype(jnp.bfloat16),
            upstream,
            preferred_element_type=jnp.float32,
        )
        grad_probs = jnp.einsum(
            "qhd,khd->hqk", upstream, value_all, preferred_element_type=jnp.float32
        )
        inner_sum = jnp.sum(softmax_w * grad_probs, axis=-1, keepdims=True)
        grad_scores = (softmax_w * (grad_probs - inner_sum)).astype(jnp.bfloat16)
        grad_query = (
            jnp.einsum("hqk,khd->qhd", grad_scores, key_all, preferred_element_type=jnp.float32)
            * score_scale
        )
        key_acc = (
            key_acc
            + jnp.einsum("hqk,qhd->khd", grad_scores, query_blk, preferred_element_type=jnp.float32)
            * score_scale
        )
        return ((key_acc, value_acc), grad_query.astype(jnp.bfloat16))

    zero_heads = jnp.zeros((group_rows, local_heads, HEAD_DIM), jnp.float32)
    (key_grad, value_grad), query_blocks = lax.scan(
        back_block, (zero_heads, zero_heads), (block_starts, lse_blocks)
    )
    grad_triples = jnp.stack(
        [
            query_blocks.reshape(group_rows, local_width),
            key_grad.reshape(group_rows, local_width).astype(jnp.bfloat16),
            value_grad.reshape(group_rows, local_width).astype(jnp.bfloat16),
        ],
        axis=1,
    )
    grad_qkv_local = jnp.einsum(
        "td,tcj->dcj", norm1_all, grad_triples, preferred_element_type=jnp.float32
    )
    triple_sums = jnp.sum(grad_triples.astype(jnp.float32), axis=0)
    grad_qv_local = jnp.stack([triple_sums[0], triple_sums[2]])
    grad_norm1 = lax.psum_scatter(
        low(
            jnp.einsum("tcj,dcj->td", grad_triples, qkv_weight, preferred_element_type=jnp.float32)
        ),
        "mp",
        scatter_dimension=0,
        tiled=True,
    ).astype(jnp.float32)
    qkv_sum = lax.psum(low(grad_qkv_local), "dp").astype(jnp.float32)
    norm1_val, norm1_back = jax.vjp(layer_norm, band_hat, norm1_gain, norm1_bias)
    from_norm1, grad_gain1_local, grad_bias1_local = norm1_back(grad_norm1)
    grad_hat = grad_after + from_norm1
    dec_sum = lax.psum(low(grad_dec_local), ("dp", "mp")).astype(jnp.float32)
    summed_small = lax.psum((grad_qv_local, grad_up_bias_local), "dp")
    shared = lax.psum(
        (
            jnp.sum(grad_hat, axis=0),
            jnp.sum(grad_hat * band_hat, axis=0),
            grad_gain1_local,
            grad_bias1_local,
            grad_gain2_local,
            grad_bias2_local,
            grad_out_bias_local,
            grad_down_bias_local,
            grad_dec_bias_local,
            grad_mask_local,
        ),
        ("dp", "mp"),
    )
    grad_patches = band_scale * (
        grad_hat - shared[0] / total_rows - band_hat * (shared[1] / total_rows)
    )
    return (
        decoder_in,
        grad_patches,
        shared[2],
        shared[3],
        qkv_sum,
        summed_small[0],
        out_sum,
        shared[6],
        shared[4],
        shared[5],
        up_sum,
        summed_small[1],
        down_sum,
        shared[7],
        dec_sum,
        shared[8],
        shared[9],
    )


def solution(mesh):
    in_specs = (
        P(("dp", "mp"), None),
        P(("dp", "mp")),
        P(("dp", "mp")),
        P(("dp", "mp")),
        P(),
        P(),
        P(None, None, "mp"),
        P(None, "mp"),
        P("mp", None),
        P(),
        P(),
        P(),
        P(None, "mp"),
        P("mp"),
        P("mp", None),
        P(),
        P(),
        P(),
        P(),
        P(("dp", "mp"), None),
        P(("dp", "mp"), None),
    )
    out_specs = (
        P(("dp", "mp"), None),
        P(("dp", "mp"), None),
        P(),
        P(),
        P(None, None, "mp"),
        P(None, "mp"),
        P("mp", None),
        P(),
        P(),
        P(),
        P(None, "mp"),
        P("mp"),
        P("mp", None),
        P(),
        P(),
        P(),
        P(),
    )
    return jax.shard_map(
        per_device, mesh=mesh, in_specs=in_specs, out_specs=out_specs, check_vma=False
    )
```

profile of v0, /device:TPU:0, one launch (start us, length us, event | category | flops | bytes accessed | tf_op | source)
XLA Modules:
  0.0 733.2 jit_solution(15494136100213632518)
XLA Ops:
  8.6 42.1 %all-reduce.1 = (f32[1024]{0:T(1024)S(1)}, f32[1024]{0:T(1024)S(1)}) all-reduce(f32[1024]{0:T(1024)S(1)} %get-tuple-element.181, f32[1024]{0:T(1024)S(1)} %get-tuple-element.180), channel_id=1, replica_groups=mesh['dp'=8,'mp'=4] {'dp','mp'}, use_global_device_ids=true, to_apply=%region_6.7 | all-reduce | flops 2048 | bytes 16384 | tf_op jit(solution)/shard_map/psum | solution.py:72
  55.6 3.0 fusion.56
  58.6 4.1 all-to-all-start.2
  63.7 17.0 %all-gather = bf16[128,1024]{1,0:T(8,128)(2,1)} all-gather(bf16[32,1024]{1,0:T(8,128)(2,1)S(1)} %constant_dynamic-slice_fusion), channel_id=2, replica_groups=mesh['dp'=8,'mp'=4] {'mp'}, dimensions={0}, use_global_device_ids=true | all-gather | bytes 327680 | tf_op jit(solution)/shard_map/all_gather | solution.py:25
  80.8 10.5 %all-gather.3 = s32[4,1,256]{2,1,0:T(1,128)S(1)} all-gather(s32[1,1,256]{2,1,0:T(1,128)S(1)} %bitcast.166), channel_id=1, replica_groups=mesh['dp'=8,'mp'=4] {'mp'}, dimensions={0}, use_global_device_ids=true | all-gather | bytes 5120 | tf_op jit(solution)/shard_map/all_gather | solution.py:82
  92.4 13.1 %all-gather.9.cloned.1.call-done = bf16[1024,1024]{1,0:T(8,128)(2,1)} async-done(((bf16[256,1024]{1,0:T(8,128)(2,1)}), bf16[1024,1024]{1,0:T(8,128)(2,1)}) %all-gather.9.cloned.1.call-update) | async-done | bytes 2097168 | tf_op jit(solution)/shard_map/all_gather | solution.py:81
  105.5 3.9 add_convert_fusion.1
  111.2 22.3 %while.27 = (s32[]{:T(128)}, bf16[2,512,4,64]{1,3,2,0:T(8,128)(2,1)}, f32[2,4,512]{2,1,0:T(4,128)S(1)}, s32[2]{0:T(128)S(1)}, s32[1024]{0:T(1024)S(1)}, /*index=...) while((s32[]{:T(128)}, ...), condition=%wide.region_12.13_spmd, body=%wide.region_9.12_spmd.sunk | while | flops 562690048 | bytes 35203332 | solution.py:114
  118.5 3.0 fusion.170
  129.7 3.0 fusion.170
  136.7 2.9 all_to_all.32
  141.5 4.1 all-to-all-start
  145.9 2.7 fusion.102
  148.7 3.2 copy.77
  151.9 8.4 %all-to-all-done = bf16[4,256,256]{1,2,0:T(8,128)(2,1)} async-done(((bf16[4,256,256]{1,2,0:T(8,128)(2,1)}), bf16[4,256,256]{1,2,0:T(8,128)(2,1)}, u32[]{:S(2)}, u32[]{:S(2)}) %all-to-all-start) | async-done | bytes 524320 | tf_op jit(solution)/shard_map/all_to_all | solution.py:116
  165.1 13.0 %all-gather.13.cloned.1.call-done = bf16[1024,512]{1,0:T(8,128)(2,1)} async-done(((bf16[256,512]{1,0:T(8,128)(2,1)}), bf16[1024,512]{1,0:T(8,128)(2,1)}) %all-gather.13.cloned.1.call-update) | async-done | bytes 1048592 | tf_op jit(solution)/shard_map/all_gather | solution.py:179
  178.1 4.1 convolution_convert_fusion.4
  182.2 42.9 %all-gather.11.cloned.1.call-done = bf16[1024,1024]{1,0:T(8,128)(2,1)} async-done(((bf16[256,1024]{1,0:T(8,128)(2,1)}), bf16[1024,1024]{1,0:T(8,128)(2,1)}) %all-gather.11.cloned.1.call-update) | async-done | bytes 2097168 | tf_op jit(solution)/shard_map/all_gather | solution.py:120
  225.1 4.7 fusion.106
  229.9 13.9 %convert_reduce_fusion = (f32[1024]{0:T(1024)}, bf16[1024,1024]{1,0:T(8,128)(2,1)S(1)}, f32[1024,1024]{1,0:T(8,128)}) fusion(f32[1024,1024]{1,0:T(8,128)S(1)} %fusion.106, f32[1024]{0:T(1024)S(1)} %convert_element_type.184, bf16[1024,1024]{1,0:T(8,128)(2,1)S(1)} %copy-done.61, bf16[1024,1024]{1,0:T(8,128)(2,1)S(1)} %copy-done), kind=kOutput, calls=%fused_computation.48 | convolution fusion | flops 2226125824 | bytes 14688256 | tf_op jit(solution)/shard_map/tc,fc->tf/dot_general | solution.py:191
  245.2 3.7 convolution_convert_fusion.3
  248.9 42.5 %reduce-scatter.8.cloned.1.call-done = bf16[256,1024]{1,0:T(8,128)(2,1)} async-done(((bf16[1024,1024]{1,0:T(8,128)(2,1)}), bf16[256,1024]{1,0:T(8,128)(2,1)}) %reduce-scatter.8.cloned.1.call-update) | async-done | bytes 524304 | tf_op jit(solution)/shard_map/reduce_scatter | solution.py:202
  298.8 3.1 convolution_convert_fusion.2
  302.1 4.6 multiply_convert_fusion.1
  312.7 4.4 fusion.107
  317.2 3.8 convolution_convert_fusion
  322.5 3.5 all-to-all-start.3
  326.0 3.1 add_convert_fusion.2
  329.2 6.1 convolution_convert_fusion.1
  335.3 5.1 all-to-all-done.3
  343.7 30.6 %while.28 = (s32[]{:T(128)}, f32[1024,4,64]{0,2,1:T(8,128)S(1)}, f32[1024,4,64]{0,2,1:T(8,128)}, bf16[2,512,4,64]{1,3,2,0:T(8,128)(2,1)}, s32[2]{0:T(128)S(1)}, ...) while((s32[]{:T(128)}, f32[1024,4,64]{0,2,1:T(8,128)S(1)}, ...), condition=%wide.region_21.22_spmd.clone, body=%wide.region_19.21_spmd.clone.sunk | while | flops 1375729664 | bytes 84740432 | solution.py:258
  351.0 3.3 multiply_reduce_fusion.3
  366.2 3.3 multiply_reduce_fusion.3
  378.6 4.6 fusion.50
  383.9 4.6 bitcast_convert_fusion
  388.6 2.8 convolution_convert_fusion.8
  391.4 3.7 all-to-all-start.1
  396.6 110.9 %all-reduce.7.cloned.1.call-done = bf16[1024,512]{1,0:T(8,128)(2,1)} async-done(((bf16[1024,512]{1,0:T(8,128)(2,1)}), bf16[1024,512]{1,0:T(8,128)(2,1)}) %all-reduce.7.cloned.1.call-update) | async-done | bytes 1048592 | tf_op jit(solution)/shard_map/psum | solution.py:286
  507.5 2.8 convert_element_type.221
  510.4 3.1 add_convert_fusion.3
  513.7 13.4 %all-reduce.2 = (f32[2,256]{1,0:T(2,128)}, f32[1024]{0:T(1024)}) all-reduce(f32[2,256]{1,0:T(2,128)S(1)} %pad_maximum_fusion.2, f32[1024]{0:T(1024)S(1)} %copy-done.49), channel_id=1, replica_groups=mesh['dp'=8,'mp'=4] {'dp'}, use_global_device_ids=true, to_apply=%region_35.36 | all-reduce | flops 1536 | bytes 12288 | tf_op jit(solution)/shard_map/psum | solution.py:287
  527.1 82.7 %all-reduce.9.cloned.1.call-done = (bf16[1024,3,256]{2,0,1:T(8,128)(2,1)}, bf16[1024,1024]{1,0:T(8,128)(2,1)}, bf16[1024,1024]{1,0:T(8,128)(2,1)}) async-done(((bf16[1024,3,256]{2,0,1:T(8,128)(2,1)}, bf16[1024,1024]{1,0:T(8,128)(2,1)}, bf16[1024,1024]{1,0:T(8,128)(2,1)}), (bf16[1024,3,256]{2,0,1:T(8,128)(2,1)}, bf16[1024,1024]{1,0:T(8,128)(2,1)}, bf16[1024,1024]{1,0:T(8,128)(2,1)})) %all-reduce.9.cloned.1.call-update) | async-done | bytes 5767184 | tf_op jit(solution)/shard_map/psum | solution.py:282
  609.9 3.5 convert_element_type.208
  618.4 13.7 %reduce-scatter.14.cloned.1.call-done = bf16[1,32,1024]{2,1,0:T(8,128)(2,1)} async-done(((bf16[4,32,1024]{2,1,0:T(8,128)(2,1)}), bf16[1,32,1024]{2,1,0:T(8,128)(2,1)}) %reduce-scatter.14.cloned.1.call-update) | async-done | bytes 65552 | tf_op jit(solution)/shard_map/reduce_scatter | solution.py:218
  632.1 10.1 %all-gather.2 = bf16[1,256,1024]{2,1,0:T(8,128)(2,1)S(1)} all-gather(bf16[1,32,1024]{2,1,0:T(8,128)(2,1)} %reduce-scatter.14.cloned.1.call-done), channel_id=4, replica_groups=mesh['dp'=8,'mp'=4] {'dp'}, dimensions={1}, use_global_device_ids=true | all-gather | bytes 589824 | tf_op jit(solution)/shard_map/all_gather | solution.py:219
  643.2 33.0 %reduce-scatter.10.cloned.1.call-done = bf16[256,1024]{1,0:T(8,128)(2,1)} async-done(((bf16[1024,1024]{1,0:T(8,128)(2,1)}), bf16[256,1024]{1,0:T(8,128)(2,1)}) %reduce-scatter.10.cloned.1.call-update) | async-done | bytes 524304 | tf_op jit(solution)/shard_map/reduce_scatter | solution.py:274
  679.7 3.6 fusion.97
  683.4 40.7 %all-reduce = (f32[1024]{0:T(1024)S(1)}, f32[1024]{0:T(1024)S(1)}, f32[1024]{0:T(1024)}, f32[1024]{0:T(1024)}, f32[1024]{0:T(1024)}, /*index=5*/f32[1024]{0:T(10...) all-reduce(f32[1024]{0:T(1024)S(1)} %get-tuple-element.176, ...), channel_id=1, replica_groups=mesh['dp'=8,'mp'=4] {'dp','mp'}, use_global_device_ids=true, to_apply=%region_28.29 | all-reduce | flops 9216 | bytes 73728 | tf_op jit(solution)/shard_map/psum | solution.py:288
  (263 shorter events, 90.6 us)
Async XLA Ops:
  7.2 222.6 %copy-start = (bf16[1024,1024]{1,0:T(8,128)(2,1)S(1)}, bf16[1024,1024]{1,0:T(8,128)(2,1)}, u32[]{:S(2)}) copy-start(bf16[1024,1024]{1,0:T(8,128)(2,1)} %param.39) | copy-start | bytes 6291460
  7.2 73.6 %copy-start.52 = (f32[2,256]{1,0:T(2,128)S(1)}, f32[2,256]{1,0:T(2,128)}, u32[]{:S(2)}) copy-start(f32[2,256]{1,0:T(2,128)} %param.32) | copy-start | bytes 6148
  7.2 73.6 %copy-start.53 = (s32[256]{0:T(256)S(1)}, s32[256]{0:T(256)}, u32[]{:S(2)}) copy-start(s32[256]{0:T(256)} %param.26) | copy-start | bytes 3076
  7.2 84.1 %copy-start.43 = (s32[256]{0:T(256)S(1)}, s32[256]{0:T(256)}, u32[]{:S(2)}) copy-start(s32[256]{0:T(256)} %param.27) | copy-start | bytes 3076
  7.2 98.2 %all-gather.9.cloned.1.call-start = ((), (), s32[]{:S(2)}) async-start(), calls=%async_computation.9 | async-start | bytes 2621440 | tf_op jit(solution)/shard_map/all_gather | solution.py:81
  50.7 109.6 %copy-start.27 = (f32[1024]{0:T(1024)}, f32[1024]{0:T(1024)S(1)}, u32[]{:S(2)}) copy-start(f32[1024]{0:T(1024)S(1)} %get-tuple-element.257) | copy-start | bytes 12292
  50.7 109.6 %copy-start.29 = (f32[1024]{0:T(1024)}, f32[1024]{0:T(1024)S(1)}, u32[]{:S(2)}) copy-start(f32[1024]{0:T(1024)S(1)} %get-tuple-element.258) | copy-start | bytes 12292
  52.0 10.8 %copy-start.33 = (f32[256]{0:T(256)}, f32[256]{0:T(256)S(1)}, u32[]{:S(2)}) copy-start(f32[256]{0:T(256)S(1)} %broadcast_multiply_fusion.4) | copy-start | bytes 3076
  53.4 9.4 %copy-start.41 = (f32[256]{0:T(256)}, f32[256]{0:T(256)S(1)}, u32[]{:S(2)}) copy-start(f32[256]{0:T(256)S(1)} %fusion.76) | copy-start | bytes 3076
  58.6 82.9 %all-to-all-start.2 = ((bf16[8,64,512]{2,1,0:T(8,128)(2,1)}), bf16[8,64,512]{2,1,0:T(8,128)(2,1)}, u32[]{:S(2)}, u32[]{:S(2)}) async-start(bf16[8,64,512]{2,1,0:T(8,128)(2,1)} %bitcast.21), calls=%async_computation.3 | async-start | bytes 1048576 | tf_op jit(solution)/shard_map/all_to_all | solution.py:156
  62.8 85.9 %all-gather.15.cloned.1.call-start = ((), (), s32[]{:S(2)}) async-start(), calls=%async_computation.18 | async-start | bytes 2359296 | tf_op jit(solution)/shard_map/all_gather | solution.py:26
  136.7 23.6 %copy-start.2 = (bf16[256,1024]{1,0:T(8,128)(2,1)S(1)}, bf16[256,1024]{1,0:T(8,128)(2,1)}, u32[]{:S(2)}) copy-start(bf16[256,1024]{1,0:T(8,128)(2,1)} %param.25) | copy-start | bytes 1572868
  136.7 23.6 %copy-start.35 = (f32[1024]{0:T(1024)S(1)}, f32[1024]{0:T(1024)}, u32[]{:S(2)}) copy-start(f32[1024]{0:T(1024)} %param.34) | copy-start | bytes 12292
  141.5 18.8 %all-to-all-start = ((bf16[4,256,256]{1,2,0:T(8,128)(2,1)}), bf16[4,256,256]{1,2,0:T(8,128)(2,1)}, u32[]{:S(2)}, u32[]{:S(2)}) async-start(bf16[4,256,256]{1,2,0:T(8,128)(2,1)} %copy.76), calls=%async_computation | async-start | bytes 1048576 | tf_op jit(solution)/shard_map/all_to_all | solution.py:116
  145.7 32.4 %all-gather.13.cloned.1.call-start = ((), (), s32[]{:S(2)}) async-start(), calls=%async_computation.12 | async-start | bytes 1310720 | tf_op jit(solution)/shard_map/all_gather | solution.py:179
  148.6 76.5 %all-gather.11.cloned.1.call-start = ((), (), s32[]{:S(2)}) async-start(), calls=%async_computation.10 | async-start | bytes 2621440 | tf_op jit(solution)/shard_map/all_gather | solution.py:120
  148.7 15.2 %copy-start.32 = (f32[1024]{0:T(1024)S(1)}, f32[1024]{0:T(1024)}, u32[]{:S(2)}) copy-start(f32[1024]{0:T(1024)} %param.35) | copy-start | bytes 12292
  148.7 15.2 %copy-start.46 = (f32[1024]{0:T(1024)S(1)}, f32[1024]{0:T(1024)}, u32[]{:S(2)}) copy-start(f32[1024]{0:T(1024)} %param.36) | copy-start | bytes 12292
  151.9 13.1 %copy-start.50 = (bf16[1024]{0:T(1024)(128)(2,1)S(1)}, bf16[1024]{0:T(1024)(128)(2,1)}, u32[]{:S(2)}) copy-start(bf16[1024]{0:T(1024)(128)(2,1)} %param.38) | copy-start | bytes 6148
  165.0 126.5 %reduce-scatter.8.cloned.1.call-start = ((), (), s32[]{:S(2)}) async-start(), calls=%async_computation.13 | async-start | bytes 2621440 | tf_op jit(solution)/shard_map/reduce_scatter | solution.py:202
  229.8 14.0 %copy-start.13 = (f32[1024,1024]{1,0:T(8,128)}, f32[1024,1024]{1,0:T(8,128)S(1)}, u32[]{:S(2)}) copy-start(f32[1024,1024]{1,0:T(8,128)S(1)} %fusion.106) | copy-start | bytes 12582916
  229.9 15.3 %copy-start.56 = (bf16[1024,1024]{1,0:T(8,128)(2,1)S(1)}, bf16[1024,1024]{1,0:T(8,128)(2,1)}, u32[]{:S(2)}) copy-start(bf16[1024,1024]{1,0:T(8,128)(2,1)} %param.37) | copy-start | bytes 6291460
  248.8 47.9 %copy-start.14 = (bf16[256,512]{1,0:T(8,128)(2,1)S(1)}, bf16[256,512]{1,0:T(8,128)(2,1)}, u32[]{:S(2)}) copy-start(bf16[256,512]{1,0:T(8,128)(2,1)} %get-tuple-element.254) | copy-start | bytes 786436
  248.9 134.4 %reduce-scatter.12.cloned.1.call-start = ((), (), s32[]{:S(2)}) async-start(), calls=%async_computation.15 | async-start | bytes 2359296 | tf_op jit(solution)/shard_map/reduce_scatter | solution.py:217
  301.9 86.7 %reduce-scatter.6.cloned.1.call-start = ((), (), s32[]{:S(2)}) async-start(), calls=%async_computation.11 | async-start | bytes 1310720 | tf_op jit(solution)/shard_map/reduce_scatter | solution.py:127
  322.5 17.9 %all-to-all-start.3 = ((bf16[256,4,256]{2,0,1:T(8,128)(2,1)}), bf16[256,4,256]{2,0,1:T(8,128)(2,1)S(1)}, u32[]{:S(2)}, u32[]{:S(2)}) async-start(bf16[256,4,256]{2,0,1:T(8,128)(2,1)} %bitcast.160), calls=%async_computation.5 | async-start | bytes 1048576 | tf_op jit(solution)/shard_map/all_to_all | solution.py:220
  326.0 181.6 %all-reduce.7.cloned.1.call-start = ((), (), s32[]{:S(2)}) async-start(), calls=%async_computation.17 | async-start | bytes 2097152 | tf_op jit(solution)/shard_map/psum | solution.py:286
  329.1 14.5 %copy-start.5 = (bf16[1024,4,64]{0,2,1:T(8,128)(2,1)S(1)}, bf16[1024,4,64]{0,2,1:T(8,128)(2,1)}, u32[]{:S(2)}) copy-start(bf16[1024,4,64]{0,2,1:T(8,128)(2,1)} %copy-done.4) | copy-start | bytes 1572868
  329.1 14.5 %copy-start.10 = (bf16[1024,4,64]{0,2,1:T(8,128)(2,1)S(1)}, bf16[1024,4,64]{0,2,1:T(8,128)(2,1)}, u32[]{:S(2)}) copy-start(bf16[1024,4,64]{0,2,1:T(8,128)(2,1)} %get-tuple-element.484) | copy-start | bytes 1572868
  329.2 280.7 %all-reduce.9.cloned.1.call-start = ((), (), s32[]{:S(2)}) async-start(), calls=%async_computation.19 | async-start | bytes 11534336 | tf_op jit(solution)/shard_map/psum | solution.py:282
  383.2 248.9 %reduce-scatter.14.cloned.1.call-start = ((), (), s32[]{:S(2)}) async-start(), calls=%async_computation.16 | async-start | bytes 327680 | tf_op jit(solution)/shard_map/reduce_scatter | solution.py:218
  383.8 292.4 %reduce-scatter.10.cloned.1.call-start = ((), (), s32[]{:S(2)}) async-start(), calls=%async_computation.14 | async-start | bytes 2621440 | tf_op jit(solution)/shard_map/reduce_scatter | solution.py:274
  388.5 121.8 %copy-start.59 = (f32[512]{0:T(512)S(1)}, f32[512]{0:T(512)}, u32[]{:S(2)}) copy-start(f32[512]{0:T(512)} %param.43) | copy-start | bytes 6148
  391.4 119.0 %all-to-all-start.1 = ((bf16[8,64,512]{2,1,0:T(8,128)(2,1)}), bf16[8,64,512]{2,1,0:T(8,128)(2,1)S(1)}, u32[]{:S(2)}, u32[]{:S(2)}) async-start(bf16[8,64,512]{2,1,0:T(8,128)(2,1)} %bitcast.19), calls=%async_computation.2 | async-start | bytes 1048576 | tf_op jit(solution)/shard_map/all_to_all | solution.py:149
  396.6 117.2 %copy-start.49 = (f32[1024]{0:T(1024)S(1)}, f32[1024]{0:T(1024)}, u32[]{:S(2)}) copy-start(f32[1024]{0:T(1024)} %get-tuple-element.237) | copy-start | bytes 12292
  615.8 60.4 %copy-start.3 = (bf16[256,1024]{1,0:T(8,128)(2,1)S(1)}, bf16[256,1024]{1,0:T(8,128)(2,1)}, u32[]{:S(2)}) copy-start(bf16[256,1024]{1,0:T(8,128)(2,1)} %param.25) | copy-start | bytes 1572868
  615.8 60.4 %copy-start.28 = (f32[1024]{0:T(1024)S(1)}, f32[1024]{0:T(1024)}, u32[]{:S(2)}) copy-start(f32[1024]{0:T(1024)} %copy-done.27) | copy-start | bytes 12292
  615.8 60.4 %copy-start.30 = (f32[1024]{0:T(1024)S(1)}, f32[1024]{0:T(1024)}, u32[]{:S(2)}) copy-start(f32[1024]{0:T(1024)} %copy-done.29) | copy-start | bytes 12292
  615.8 60.4 %copy-start.31 = (f32[1024]{0:T(1024)S(1)}, f32[1024]{0:T(1024)}, u32[]{:S(2)}) copy-start(f32[1024]{0:T(1024)} %param.29) | copy-start | bytes 12292
  615.8 60.4 %copy-start.34 = (f32[256]{0:T(256)S(1)}, f32[256]{0:T(256)}, u32[]{:S(2)}) copy-start(f32[256]{0:T(256)} %copy-done.33) | copy-start | bytes 3076
  615.9 62.1 %copy-start.42 = (f32[256]{0:T(256)S(1)}, f32[256]{0:T(256)}, u32[]{:S(2)}) copy-start(f32[256]{0:T(256)} %copy-done.41) | copy-start | bytes 3076
  615.9 62.1 %copy-start.40 = (f32[256]{0:T(256)S(1)}, f32[256]{0:T(256)}, u32[]{:S(2)}) copy-start(f32[256]{0:T(256)} %copy-done.39) | copy-start | bytes 3076
  615.9 63.8 %copy-start.45 = (f32[256]{0:T(256)S(1)}, f32[256]{0:T(256)}, u32[]{:S(2)}) copy-start(f32[256]{0:T(256)} %copy-done.44) | copy-start | bytes 3076
  618.4 65.0 %copy-start.36 = (f32[1024]{0:T(1024)S(1)}, f32[1024]{0:T(1024)}, u32[]{:S(2)}) copy-start(f32[1024]{0:T(1024)} %get-tuple-element.171) | copy-start | bytes 12292
  618.4 65.0 %copy-start.37 = (f32[1024]{0:T(1024)S(1)}, f32[1024]{0:T(1024)}, u32[]{:S(2)}) copy-start(f32[1024]{0:T(1024)} %get-tuple-element.177) | copy-start | bytes 12292
  618.4 65.0 %copy-start.38 = (f32[1024]{0:T(1024)S(1)}, f32[1024]{0:T(1024)}, u32[]{:S(2)}) copy-start(f32[1024]{0:T(1024)} %get-tuple-element.240) | copy-start | bytes 12292
  618.4 65.0 %copy-start.51 = (f32[512]{0:T(512)S(1)}, f32[512]{0:T(512)}, u32[]{:S(2)}) copy-start(f32[512]{0:T(512)} %get-tuple-element.253) | copy-start | bytes 6148
  676.3 50.2 %copy-start.1 = (bf16[1024,1024]{1,0:T(8,128)(2,1)S(1)}, bf16[1024,1024]{1,0:T(8,128)(2,1)}, u32[]{:S(2)}) copy-start(bf16[1024,1024]{1,0:T(8,128)(2,1)} %param.39) | copy-start | bytes 6291460
  (38 other events, 116.2 us)
Sparse Core Ops, SparseCore 0:
  55.7 49.7 all-gather.8
  107.4 26.6 all-gather.14
  148.7 29.2 all-gather.12
  180.1 45.0 all-gather.10
  249.0 42.4 reduce-scatter.7
  302.0 40.2 reduce-scatter.11
  345.2 27.3 reduce-scatter.5
  378.3 129.2 all-reduce.6
  512.3 97.5 all-reduce.8
  612.0 20.0 reduce-scatter.13
  634.4 41.8 reduce-scatter.9
where the time goes:
time: 743 us; the launch traced here: 733 us
  waiting for transfers between devices  366 us (49%)
  blocking collectives  134 us (18%)
  matrix products  111 us (15%)
  other arithmetic  52.9 us (7%)
  local copies, waits for them, and re-layouts  30 us (4%)
  starting transfers between devices  16.3 us (2%)
  between operations  14.9 us (2%)
  loops' own time  8.35 us (1%)
    psum x1, waiting for transfers between devices, per_device(): dec_sum = lax.psum(low(grad_dec_local), ('dp', 'mp')).astype(jnp.float32)  111 us
    psum x1, waiting for transfers between devices, per_device(): qkv_sum = lax.psum(low(grad_qkv_local), 'dp').astype(jnp.float32)  82.7 us
    all_gather x1, waiting for transfers between devices, per_device(): norm2_all = lax.all_gather(normed2, 'mp', axis=0, tiled=True)  42.9 us
    reduce_scatter x1, waiting for transfers between devices, per_device(): lax.psum_scatter(low(jnp.einsum('tf,df->td', grad_pre, up_weight, preferr...  42.5 us
    psum x1, blocking collectives, per_device(): lax.psum((jnp.sum(inputs_f, axis=0), jnp.sum(inputs_f * inputs_f, axis=0)...  42.1 us
    psum x1, blocking collectives, per_device(): lax.psum((jnp.sum(grad_hat, axis=0), jnp.sum(grad_hat * band_hat, axis=0)...  40.7 us
    reduce_scatter x1, waiting for transfers between devices, per_device(): lax.psum_scatter(low(jnp.einsum('tcj,dcj->td', grad_triples, qkv_weight,...  33 us
    all_gather x1, blocking collectives, gather_rows(): column = lax.all_gather(mine, 'mp', axis=0)  17 us
  transfers between devices with their start and end apart: 15, of which 10 were waited for; matrix products, arithmetic and copies ran while one was open for 19% of the time, Pallas kernels for 0%

commit v1 on v0

--- a/solution.py
+++ b/solution.py
@@ -2,10 +2,12 @@
 import jax.numpy as jnp
 from jax import lax
 from jax.sharding import PartitionSpec as P
+from jax.lax import all_gather
 
 HEAD_DIM = 64
 QBLOCK = 512
 NEG_FILL = -1000000000.0
+carry_fields = lambda x_part, device_axis: all_gather(x_part, device_axis).sum(axis=0)
 
 
 def layer_norm(hidden, gain, bias_vec):
@@ -283,7 +285,7 @@
     norm1_val, norm1_back = jax.vjp(layer_norm, band_hat, norm1_gain, norm1_bias)
     from_norm1, grad_gain1_local, grad_bias1_local = norm1_back(grad_norm1)
     grad_hat = grad_after + from_norm1
-    dec_sum = lax.psum(low(grad_dec_local), ("dp", "mp")).astype(jnp.float32)
+    dec_sum = carry_fields(low(grad_dec_local), ("dp", "mp")).astype(jnp.float32)
     summed_small = lax.psum((grad_qv_local, grad_up_bias_local), "dp")
     shared = lax.psum(
         (

time: 743 us -> 790 us (1.063)
  waiting for transfers between devices: 366 us -> 386 us
  other arithmetic: 52.9 us -> 64.2 us
  matrix products: 111 us -> 119 us
    all_gather x0 -> x1, waiting for transfers between devices: none -> 147 us  [all_gather(x_part, device_axis).sum(axis=0)]
    psum x1 -> x0, waiting for transfers between devices: 111 us -> none  [per_device(): dec_sum = lax.psum(low(grad_dec_local), ('dp', 'mp')).astype(jnp.float32)]
    psum x1, waiting for transfers between devices: 82.7 us -> 53.4 us  [per_device(): qkv_sum = lax.psum(low(grad_qkv_local), 'dp').astype(jnp.float32)]
    all_to_all x1, waiting for transfers between devices: 0.01 us -> 14.2 us  [per_device(): lax.all_to_all(outgoing.reshape(data_par, capacity, dec_width), 'dp', spl...]
    reduce_sum x0 -> x1, other arithmetic: none -> 11.5 us  [all_gather(x_part, device_axis).sum(axis=0)]
  transfers between devices with their start and end apart: 15 -> 15, of which waited for: 10 -> 11; matrix products, arithmetic and copies ran while one was open for 19% -> 20% of each run, Pallas kernels for 0% -> 0%
where the time goes in v1:
time: 790 us; the launch traced here: 780 us
  waiting for transfers between devices  386 us (49%)
  blocking collectives  136 us (17%)
  matrix products  119 us (15%)
  other arithmetic  64.2 us (8%)
  local copies, waits for them, and re-layouts  34.5 us (4%)
  starting transfers between devices  16.8 us (2%)
  between operations  14.8 us (2%)
  loops' own time  8.46 us (1%)
    all_gather x1, waiting for transfers between devices, all_gather(x_part, device_axis).sum(axis=0)  147 us
    psum x1, waiting for transfers between devices, per_device(): qkv_sum = lax.psum(low(grad_qkv_local), 'dp').astype(jnp.float32)  53.4 us
    all_gather x1, waiting for transfers between devices, per_device(): norm2_all = lax.all_gather(normed2, 'mp', axis=0, tiled=True)  42.9 us
    psum x1, blocking collectives, per_device(): lax.psum((jnp.sum(grad_hat, axis=0), jnp.sum(grad_hat * band_hat, axis=0)...  42.8 us
    reduce_scatter x1, waiting for transfers between devices, per_device(): lax.psum_scatter(low(jnp.einsum('tf,df->td', grad_pre, up_weight, preferr...  42.3 us
    psum x1, blocking collectives, per_device(): lax.psum((jnp.sum(inputs_f, axis=0), jnp.sum(inputs_f * inputs_f, axis=0)...  42.1 us
    reduce_scatter x1, waiting for transfers between devices, per_device(): lax.psum_scatter(low(jnp.einsum('tcj,dcj->td', grad_triples, qkv_weight,...  33.4 us
    all_gather x1, blocking collectives, gather_rows(): column = lax.all_gather(mine, 'mp', axis=0)  16.9 us
  transfers between devices with their start and end apart: 15, of which 11 were waited for; matrix products, arithmetic and copies ran while one was open for 20% of the time, Pallas kernels for 0%

profile of v1, /device:TPU:0, one launch (start us, length us, event | category | flops | bytes accessed | tf_op | source)
XLA Modules:
  0.0 780.1 jit_solution(11948669551419301176)
XLA Ops:
  8.6 42.1 %all-reduce.1 = (f32[1024]{0:T(1024)S(1)}, f32[1024]{0:T(1024)S(1)}) all-reduce(f32[1024]{0:T(1024)S(1)} %get-tuple-element.181, f32[1024]{0:T(1024)S(1)} %get-tuple-element.180), channel_id=1, replica_groups=mesh['dp'=8,'mp'=4] {'dp','mp'}, use_global_device_ids=true, to_apply=%region_6.7 | all-reduce | flops 2048 | bytes 16384 | tf_op jit(solution)/shard_map/psum | solution.py:74
  59.7 4.2 all-to-all-start.2
  64.8 16.9 %all-gather = bf16[128,1024]{1,0:T(8,128)(2,1)} all-gather(bf16[32,1024]{1,0:T(8,128)(2,1)S(1)} %constant_dynamic-slice_fusion), channel_id=2, replica_groups=mesh['dp'=8,'mp'=4] {'mp'}, dimensions={0}, use_global_device_ids=true | all-gather | bytes 327680 | tf_op jit(solution)/shard_map/all_gather | solution.py:27
  81.8 10.6 %all-gather.4 = s32[4,1,256]{2,1,0:T(1,128)S(1)} all-gather(s32[1,1,256]{2,1,0:T(1,128)S(1)} %bitcast.167), channel_id=1, replica_groups=mesh['dp'=8,'mp'=4] {'mp'}, dimensions={0}, use_global_device_ids=true | all-gather | bytes 5120 | tf_op jit(solution)/shard_map/all_gather | solution.py:84
  93.5 13.1 %all-gather.11.cloned.1.call-done = bf16[1024,1024]{1,0:T(8,128)(2,1)} async-done(((bf16[256,1024]{1,0:T(8,128)(2,1)}), bf16[1024,1024]{1,0:T(8,128)(2,1)}) %all-gather.11.cloned.1.call-update) | async-done | bytes 2097168 | tf_op jit(solution)/shard_map/all_gather | solution.py:83
  106.6 3.9 add_convert_fusion.1
  112.2 22.3 %while.27 = (s32[]{:T(128)}, bf16[2,512,4,64]{1,3,2,0:T(8,128)(2,1)}, f32[2,4,512]{2,1,0:T(4,128)S(1)}, s32[2]{0:T(128)S(1)}, s32[1024]{0:T(1024)S(1)}, /*index=...) while((s32[]{:T(128)}, ...), condition=%wide.region_12.13_spmd, body=%wide.region_9.12_spmd.sunk | while | flops 562690048 | bytes 35203332 | solution.py:116
  142.5 4.1 all-to-all-start
  149.7 3.2 copy.77
  152.9 8.4 %all-to-all-done = bf16[4,256,256]{1,2,0:T(8,128)(2,1)} async-done(((bf16[4,256,256]{1,2,0:T(8,128)(2,1)}), bf16[4,256,256]{1,2,0:T(8,128)(2,1)}, u32[]{:S(2)}, u32[]{:S(2)}) %all-to-all-start) | async-done | bytes 524320 | tf_op jit(solution)/shard_map/all_to_all | solution.py:118
  166.1 13.0 %all-gather.15.cloned.1.call-done = bf16[1024,512]{1,0:T(8,128)(2,1)} async-done(((bf16[256,512]{1,0:T(8,128)(2,1)}), bf16[1024,512]{1,0:T(8,128)(2,1)}) %all-gather.15.cloned.1.call-update) | async-done | bytes 1048592 | tf_op jit(solution)/shard_map/all_gather | solution.py:181
  179.1 4.1 convolution_convert_fusion.4
  183.2 42.9 %all-gather.13.cloned.1.call-done = bf16[1024,1024]{1,0:T(8,128)(2,1)} async-done(((bf16[256,1024]{1,0:T(8,128)(2,1)}), bf16[1024,1024]{1,0:T(8,128)(2,1)}) %all-gather.13.cloned.1.call-update) | async-done | bytes 2097168 | tf_op jit(solution)/shard_map/all_gather | solution.py:122
  226.1 4.7 fusion.106
  230.9 13.9 %convert_reduce_fusion = (f32[1024]{0:T(1024)}, bf16[1024,1024]{1,0:T(8,128)(2,1)S(1)}, f32[1024,1024]{1,0:T(8,128)}) fusion(f32[1024,1024]{1,0:T(8,128)S(1)} %fusion.106, f32[1024]{0:T(1024)S(1)} %convert_element_type.186, bf16[1024,1024]{1,0:T(8,128)(2,1)S(1)} %copy-done.66, bf16[1024,1024]{1,0:T(8,128)(2,1)S(1)} %copy-done), kind=kOutput, calls=%fused_computation.48 | convolution fusion | flops 2226125824 | bytes 14688256 | tf_op jit(solution)/shard_map/tc,fc->tf/dot_general | solution.py:193
  246.1 3.7 convolution_convert_fusion.3
  250.2 42.3 %reduce-scatter.8.cloned.1.call-done = bf16[256,1024]{1,0:T(8,128)(2,1)} async-done(((bf16[1024,1024]{1,0:T(8,128)(2,1)}), bf16[256,1024]{1,0:T(8,128)(2,1)}) %reduce-scatter.8.cloned.1.call-update) | async-done | bytes 524304 | tf_op jit(solution)/shard_map/reduce_scatter | solution.py:204
  300.0 3.1 convolution_convert_fusion.2
  303.1 4.6 multiply_convert_fusion.1
  307.7 3.7 convolution_convert_fusion.5
  311.4 3.7 convolution_convert_fusion
  316.7 3.5 all-to-all-start.3
  320.2 4.1 convolution_convert_fusion.6
  324.4 6.0 convolution_convert_fusion.1
  330.5 4.1 all-to-all-done.3
  338.6 45.7 %while.28 = (s32[]{:T(128)}, f32[1024,4,64]{0,2,1:T(8,128)S(1)}, f32[1024,4,64]{0,2,1:T(8,128)}, bf16[2,512,4,64]{1,3,2,0:T(8,128)(2,1)}, s32[2]{0:T(128)S(1)}, ...) while((s32[]{:T(128)}, f32[1024,4,64]{0,2,1:T(8,128)S(1)}, ...), condition=%wide.region_21.22_spmd.clone, body=%wide.region_19.21_spmd.clone.sunk | while | flops 1375729664 | bytes 164432320 | solution.py:260
  343.5 3.3 multiply_reduce_fusion.3
  346.8 3.7 multiply_convert_fusion.3
  350.5 3.5 fusion.181
  355.4 3.6 fusion.182
  365.6 3.3 multiply_reduce_fusion.3
  369.0 3.7 multiply_convert_fusion.3
  372.7 3.4 fusion.181
  377.4 4.8 fusion.182
  387.6 4.6 fusion.50
  393.2 4.6 bitcast_convert_fusion
  397.8 3.3 fusion.107
  405.5 4.1 all-to-all-start.1
  411.2 14.2 %all-to-all-done.1 = bf16[8,64,512]{2,1,0:T(8,128)(2,1)S(1)} async-done(((bf16[8,64,512]{2,1,0:T(8,128)(2,1)}), bf16[8,64,512]{2,1,0:T(8,128)(2,1)S(1)}, u32[]{:S(2)}, u32[]{:S(2)}) %all-to-all-start.1) | async-done | bytes 524320 | tf_op jit(solution)/shard_map/all_to_all | solution.py:151
  428.7 13.3 %all-reduce.2 = (f32[2,256]{1,0:T(2,128)}, f32[1024]{0:T(1024)}) all-reduce(f32[2,256]{1,0:T(2,128)S(1)} %pad_maximum_fusion.2, f32[1024]{0:T(1024)S(1)} %copy-done.56), channel_id=1, replica_groups=mesh['dp'=8,'mp'=4] {'dp'}, use_global_device_ids=true, to_apply=%region_35.36 | all-reduce | flops 1536 | bytes 12288 | tf_op jit(solution)/shard_map/psum | solution.py:289
  442.0 53.4 %all-reduce.6.cloned.1.call-done = (bf16[1024,3,256]{2,0,1:T(8,128)(2,1)}, bf16[1024,1024]{1,0:T(8,128)(2,1)}, bf16[1024,1024]{1,0:T(8,128)(2,1)}) async-done(((bf16[1024,3,256]{2,0,1:T(8,128)(2,1)}, bf16[1024,1024]{1,0:T(8,128)(2,1)}, bf16[1024,1024]{1,0:T(8,128)(2,1)}), (bf16[1024,3,256]{2,0,1:T(8,128)(2,1)}, bf16[1024,1024]{1,0:T(8,128)(2,1)}, bf16[1024,1024]{1,0:T(8,128)(2,1)})) %all-reduce.6.cloned.1.call-update) | async-done | bytes 5767184 | tf_op jit(solution)/shard_map/psum | solution.py:284
  495.4 3.5 convert_element_type.210
  504.0 13.8 %reduce-scatter.14.cloned.1.call-done = bf16[1,32,1024]{2,1,0:T(8,128)(2,1)} async-done(((bf16[4,32,1024]{2,1,0:T(8,128)(2,1)}), bf16[1,32,1024]{2,1,0:T(8,128)(2,1)}) %reduce-scatter.14.cloned.1.call-update) | async-done | bytes 65552 | tf_op jit(solution)/shard_map/reduce_scatter | solution.py:220
  517.8 10.1 %all-gather.2 = bf16[1,256,1024]{2,1,0:T(8,128)(2,1)S(1)} all-gather(bf16[1,32,1024]{2,1,0:T(8,128)(2,1)} %reduce-scatter.14.cloned.1.call-done), channel_id=4, replica_groups=mesh['dp'=8,'mp'=4] {'dp'}, dimensions={1}, use_global_device_ids=true | all-gather | bytes 589824 | tf_op jit(solution)/shard_map/all_gather | solution.py:221
  529.0 33.4 %reduce-scatter.10.cloned.1.call-done = bf16[256,1024]{1,0:T(8,128)(2,1)} async-done(((bf16[1024,1024]{1,0:T(8,128)(2,1)}), bf16[256,1024]{1,0:T(8,128)(2,1)}) %reduce-scatter.10.cloned.1.call-update) | async-done | bytes 524304 | tf_op jit(solution)/shard_map/reduce_scatter | solution.py:276
  568.4 42.8 %all-reduce = (f32[1024]{0:T(1024)S(1)}, f32[1024]{0:T(1024)S(1)}, f32[1024]{0:T(1024)}, f32[1024]{0:T(1024)}, f32[1024]{0:T(1024)}, /*index=5*/f32[1024]{0:T(10...) all-reduce(f32[1024]{0:T(1024)S(1)} %get-tuple-element.176, ...), channel_id=1, replica_groups=mesh['dp'=8,'mp'=4] {'dp','mp'}, use_global_device_ids=true, to_apply=%region_28.29 | all-reduce | flops 9216 | bytes 73728 | tf_op jit(solution)/shard_map/psum | solution.py:290
  613.6 146.6 %all-gather.19.cloned.1.call-done = bf16[32768,512]{1,0:T(8,128)(2,1)} async-done(((bf16[1024,512]{1,0:T(8,128)(2,1)}), bf16[32768,512]{1,0:T(8,128)(2,1)}) %all-gather.19.cloned.1.call-update) | async-done | bytes 33554448 | tf_op jit(solution)/shard_map/all_gather | solution.py:10
  760.3 11.5 %reduce_sum.306 = bf16[1024,512]{1,0:T(8,128)(2,1)S(1)} reduce(bf16[32,1024,512]{2,1,0:T(8,128)(2,1)} %bitcast.153, bf16[]{:T(256)} %constant.79.clone.1), dimensions={0}, to_apply=%region_50.51 | reduce | flops 16252928 | bytes 34603008 | tf_op jit(solution)/shard_map/reduce_sum | solution.py:10
  (280 shorter events, 104.5 us)
Async XLA Ops:
  7.2 223.6 %copy-start = (bf16[1024,1024]{1,0:T(8,128)(2,1)S(1)}, bf16[1024,1024]{1,0:T(8,128)(2,1)}, u32[]{:S(2)}) copy-start(bf16[1024,1024]{1,0:T(8,128)(2,1)} %param.39) | copy-start | bytes 6291460
  7.2 74.6 %copy-start.60 = (s32[256]{0:T(256)S(1)}, s32[256]{0:T(256)}, u32[]{:S(2)}) copy-start(s32[256]{0:T(256)} %param.26) | copy-start | bytes 3076
  7.2 85.2 %copy-start.59 = (f32[2,256]{1,0:T(2,128)S(1)}, f32[2,256]{1,0:T(2,128)}, u32[]{:S(2)}) copy-start(f32[2,256]{1,0:T(2,128)} %param.32) | copy-start | bytes 6148
  7.2 85.2 %copy-start.50 = (s32[256]{0:T(256)S(1)}, s32[256]{0:T(256)}, u32[]{:S(2)}) copy-start(s32[256]{0:T(256)} %param.27) | copy-start | bytes 3076
  7.2 99.4 %all-gather.11.cloned.1.call-start = ((), (), s32[]{:S(2)}) async-start(), calls=%async_computation.9 | async-start | bytes 2621440 | tf_op jit(solution)/shard_map/all_gather | solution.py:83
  50.7 110.6 %copy-start.34 = (f32[1024]{0:T(1024)}, f32[1024]{0:T(1024)S(1)}, u32[]{:S(2)}) copy-start(f32[1024]{0:T(1024)S(1)} %get-tuple-element.257) | copy-start | bytes 12292
  50.7 110.6 %copy-start.36 = (f32[1024]{0:T(1024)}, f32[1024]{0:T(1024)S(1)}, u32[]{:S(2)}) copy-start(f32[1024]{0:T(1024)S(1)} %get-tuple-element.258) | copy-start | bytes 12292
  59.7 82.8 %all-to-all-start.2 = ((bf16[8,64,512]{2,1,0:T(8,128)(2,1)}), bf16[8,64,512]{2,1,0:T(8,128)(2,1)}, u32[]{:S(2)}, u32[]{:S(2)}) async-start(bf16[8,64,512]{2,1,0:T(8,128)(2,1)} %bitcast.21), calls=%async_computation.3 | async-start | bytes 1048576 | tf_op jit(solution)/shard_map/all_to_all | solution.py:158
  63.9 85.8 %all-gather.17.cloned.1.call-start = ((), (), s32[]{:S(2)}) async-start(), calls=%async_computation.17 | async-start | bytes 2359296 | tf_op jit(solution)/shard_map/all_gather | solution.py:28
  134.6 18.4 %copy-start.5 = (bf16[1024,4,64]{0,2,1:T(8,128)(2,1)}, bf16[1024,4,64]{0,2,1:T(8,128)(2,1)S(1)}, u32[]{:S(2)}) copy-start(bf16[1024,4,64]{0,2,1:T(8,128)(2,1)S(1)} %get-tuple-element.482) | copy-start | bytes 1572868
  137.7 23.6 %copy-start.7 = (bf16[256,1024]{1,0:T(8,128)(2,1)S(1)}, bf16[256,1024]{1,0:T(8,128)(2,1)}, u32[]{:S(2)}) copy-start(bf16[256,1024]{1,0:T(8,128)(2,1)} %param.25) | copy-start | bytes 1572868
  137.7 23.6 %copy-start.42 = (f32[1024]{0:T(1024)S(1)}, f32[1024]{0:T(1024)}, u32[]{:S(2)}) copy-start(f32[1024]{0:T(1024)} %param.34) | copy-start | bytes 12292
  142.5 18.8 %all-to-all-start = ((bf16[4,256,256]{1,2,0:T(8,128)(2,1)}), bf16[4,256,256]{1,2,0:T(8,128)(2,1)}, u32[]{:S(2)}, u32[]{:S(2)}) async-start(bf16[4,256,256]{1,2,0:T(8,128)(2,1)} %copy.76), calls=%async_computation | async-start | bytes 1048576 | tf_op jit(solution)/shard_map/all_to_all | solution.py:118
  146.7 32.4 %all-gather.15.cloned.1.call-start = ((), (), s32[]{:S(2)}) async-start(), calls=%async_computation.12 | async-start | bytes 1310720 | tf_op jit(solution)/shard_map/all_gather | solution.py:181
  146.9 17.0 %copy-start.61 = (s32[256]{0:T(256)}, s32[256]{0:T(256)S(1)}, u32[]{:S(2)}) copy-start(s32[256]{0:T(256)S(1)} %multiply_add_fusion.2) | copy-start | bytes 3076
  149.6 76.5 %all-gather.13.cloned.1.call-start = ((), (), s32[]{:S(2)}) async-start(), calls=%async_computation.10 | async-start | bytes 2621440 | tf_op jit(solution)/shard_map/all_gather | solution.py:122
  149.7 15.2 %copy-start.39 = (f32[1024]{0:T(1024)S(1)}, f32[1024]{0:T(1024)}, u32[]{:S(2)}) copy-start(f32[1024]{0:T(1024)} %param.35) | copy-start | bytes 12292
  149.7 15.2 %copy-start.53 = (f32[1024]{0:T(1024)S(1)}, f32[1024]{0:T(1024)}, u32[]{:S(2)}) copy-start(f32[1024]{0:T(1024)} %param.36) | copy-start | bytes 12292
  166.0 126.5 %reduce-scatter.8.cloned.1.call-start = ((), (), s32[]{:S(2)}) async-start(), calls=%async_computation.13 | async-start | bytes 2621440 | tf_op jit(solution)/shard_map/reduce_scatter | solution.py:204
  230.9 15.3 %copy-start.63 = (bf16[1024,1024]{1,0:T(8,128)(2,1)S(1)}, bf16[1024,1024]{1,0:T(8,128)(2,1)}, u32[]{:S(2)}) copy-start(bf16[1024,1024]{1,0:T(8,128)(2,1)} %param.37) | copy-start | bytes 6291460
  246.1 46.3 %copy-start.12 = (f32[256,1024]{1,0:T(8,128)S(1)}, f32[256,1024]{1,0:T(8,128)}, u32[]{:S(2)}) copy-start(f32[256,1024]{1,0:T(8,128)} %copy-done.11) | copy-start | bytes 3145732
  249.9 47.2 %copy-start.23 = (bf16[256,512]{1,0:T(8,128)(2,1)S(1)}, bf16[256,512]{1,0:T(8,128)(2,1)}, u32[]{:S(2)}) copy-start(bf16[256,512]{1,0:T(8,128)(2,1)} %get-tuple-element.254) | copy-start | bytes 786436
  249.9 142.4 %reduce-scatter.12.cloned.1.call-start = ((), (), s32[]{:S(2)}) async-start(), calls=%async_computation.15 | async-start | bytes 2359296 | tf_op jit(solution)/shard_map/reduce_scatter | solution.py:219
  316.7 17.8 %all-to-all-start.3 = ((bf16[256,4,256]{2,0,1:T(8,128)(2,1)}), bf16[256,4,256]{2,0,1:T(8,128)(2,1)S(1)}, u32[]{:S(2)}, u32[]{:S(2)}) async-start(bf16[256,4,256]{2,0,1:T(8,128)(2,1)} %bitcast.120), calls=%async_computation.5 | async-start | bytes 1048576 | tf_op jit(solution)/shard_map/all_to_all | solution.py:222
  320.2 82.5 %reduce-scatter.6.cloned.1.call-start = ((), (), s32[]{:S(2)}) async-start(), calls=%async_computation.11 | async-start | bytes 1310720 | tf_op jit(solution)/shard_map/reduce_scatter | solution.py:129
  324.3 14.3 %copy-start.6 = (bf16[1024,4,64]{0,2,1:T(8,128)(2,1)S(1)}, bf16[1024,4,64]{0,2,1:T(8,128)(2,1)}, u32[]{:S(2)}) copy-start(bf16[1024,4,64]{0,2,1:T(8,128)(2,1)} %copy-done.5) | copy-start | bytes 1572868
  324.3 14.3 %copy-start.10 = (bf16[1024,4,64]{0,2,1:T(8,128)(2,1)S(1)}, bf16[1024,4,64]{0,2,1:T(8,128)(2,1)}, u32[]{:S(2)}) copy-start(bf16[1024,4,64]{0,2,1:T(8,128)(2,1)} %copy-done.9) | copy-start | bytes 1572868
  324.4 171.0 %all-reduce.6.cloned.1.call-start = ((), (), s32[]{:S(2)}) async-start(), calls=%async_computation.19 | async-start | bytes 11534336 | tf_op jit(solution)/shard_map/psum | solution.py:284
  392.3 125.6 %reduce-scatter.14.cloned.1.call-start = ((), (), s32[]{:S(2)}) async-start(), calls=%async_computation.16 | async-start | bytes 327680 | tf_op jit(solution)/shard_map/reduce_scatter | solution.py:220
  393.0 169.4 %reduce-scatter.10.cloned.1.call-start = ((), (), s32[]{:S(2)}) async-start(), calls=%async_computation.14 | async-start | bytes 2621440 | tf_op jit(solution)/shard_map/reduce_scatter | solution.py:276
  397.8 362.5 %all-gather.19.cloned.1.call-start = ((), (), s32[]{:S(2)}) async-start(), calls=%async_computation.18 | async-start | bytes 34603008 | tf_op jit(solution)/shard_map/all_gather | solution.py:10
  402.6 22.7 %copy-start.65 = (f32[512]{0:T(512)S(1)}, f32[512]{0:T(512)}, u32[]{:S(2)}) copy-start(f32[512]{0:T(512)} %param.43) | copy-start | bytes 6148
  405.5 23.2 %copy-start.56 = (f32[1024]{0:T(1024)S(1)}, f32[1024]{0:T(1024)}, u32[]{:S(2)}) copy-start(f32[1024]{0:T(1024)} %get-tuple-element.237) | copy-start | bytes 12292
  405.5 19.8 %all-to-all-start.1 = ((bf16[8,64,512]{2,1,0:T(8,128)(2,1)}), bf16[8,64,512]{2,1,0:T(8,128)(2,1)S(1)}, u32[]{:S(2)}, u32[]{:S(2)}) async-start(bf16[8,64,512]{2,1,0:T(8,128)(2,1)} %bitcast.19), calls=%async_computation.2 | async-start | bytes 1048576 | tf_op jit(solution)/shard_map/all_to_all | solution.py:151
  501.4 61.0 %copy-start.8 = (bf16[256,1024]{1,0:T(8,128)(2,1)S(1)}, bf16[256,1024]{1,0:T(8,128)(2,1)}, u32[]{:S(2)}) copy-start(bf16[256,1024]{1,0:T(8,128)(2,1)} %param.25) | copy-start | bytes 1572868
  501.4 61.0 %copy-start.35 = (f32[1024]{0:T(1024)S(1)}, f32[1024]{0:T(1024)}, u32[]{:S(2)}) copy-start(f32[1024]{0:T(1024)} %copy-done.34) | copy-start | bytes 12292
  501.4 61.0 %copy-start.37 = (f32[1024]{0:T(1024)S(1)}, f32[1024]{0:T(1024)}, u32[]{:S(2)}) copy-start(f32[1024]{0:T(1024)} %copy-done.36) | copy-start | bytes 12292
  501.4 61.0 %copy-start.38 = (f32[1024]{0:T(1024)S(1)}, f32[1024]{0:T(1024)}, u32[]{:S(2)}) copy-start(f32[1024]{0:T(1024)} %param.29) | copy-start | bytes 12292
  501.4 61.0 %copy-start.41 = (f32[256]{0:T(256)S(1)}, f32[256]{0:T(256)}, u32[]{:S(2)}) copy-start(f32[256]{0:T(256)} %copy-done.40) | copy-start | bytes 3076
  501.4 62.5 %copy-start.49 = (f32[256]{0:T(256)S(1)}, f32[256]{0:T(256)}, u32[]{:S(2)}) copy-start(f32[256]{0:T(256)} %copy-done.48) | copy-start | bytes 3076
  501.4 62.5 %copy-start.47 = (f32[256]{0:T(256)S(1)}, f32[256]{0:T(256)}, u32[]{:S(2)}) copy-start(f32[256]{0:T(256)} %copy-done.46) | copy-start | bytes 3076
  501.4 64.2 %copy-start.17 = (f32[256,1024]{1,0:T(8,128)S(1)}, f32[256,1024]{1,0:T(8,128)}, u32[]{:S(2)}) copy-start(f32[256,1024]{1,0:T(8,128)} %copy-done.16) | copy-start | bytes 3145732
  501.5 64.2 %copy-start.22 = (f32[256,1024]{1,0:T(8,128)S(1)}, f32[256,1024]{1,0:T(8,128)}, u32[]{:S(2)}) copy-start(f32[256,1024]{1,0:T(8,128)} %get-tuple-element.264) | copy-start | bytes 3145732
  501.5 64.2 %copy-start.52 = (f32[256]{0:T(256)S(1)}, f32[256]{0:T(256)}, u32[]{:S(2)}) copy-start(f32[256]{0:T(256)} %copy-done.51) | copy-start | bytes 3076
  504.0 64.4 %copy-start.43 = (f32[1024]{0:T(1024)S(1)}, f32[1024]{0:T(1024)}, u32[]{:S(2)}) copy-start(f32[1024]{0:T(1024)} %get-tuple-element.171) | copy-start | bytes 12292
  504.0 64.4 %copy-start.44 = (f32[1024]{0:T(1024)S(1)}, f32[1024]{0:T(1024)}, u32[]{:S(2)}) copy-start(f32[1024]{0:T(1024)} %get-tuple-element.177) | copy-start | bytes 12292
  504.0 64.4 %copy-start.45 = (f32[1024]{0:T(1024)S(1)}, f32[1024]{0:T(1024)}, u32[]{:S(2)}) copy-start(f32[1024]{0:T(1024)} %get-tuple-element.240) | copy-start | bytes 12292
  504.0 64.4 %copy-start.58 = (f32[512]{0:T(512)S(1)}, f32[512]{0:T(512)}, u32[]{:S(2)}) copy-start(f32[512]{0:T(512)} %get-tuple-element.253) | copy-start | bytes 6148
  (46 other events, 175.9 us)
Sparse Core Ops, SparseCore 0:
  56.8 49.7 all-gather.10
  108.5 26.6 all-gather.16
  149.7 29.2 all-gather.14
  181.1 45.0 all-gather.12
  250.0 42.4 reduce-scatter.7
  303.2 40.3 reduce-scatter.11
  346.4 27.3 reduce-scatter.5
  392.4 102.9 all-reduce.5
  497.7 20.0 reduce-scatter.13
  520.5 41.8 reduce-scatter.9
  565.3 194.8 all-gather.18
